TPU v7x, 32 devices: a whole 2x2x4 slice. The times are simulated.
32 devices in a mesh: groups: 2 (over y), ctx: 4 (over z), head: 2 (over x), row: 2 (over core).
Axes of the slice: x: 2, y: 2, z: 4, core: 2. Of those that a mesh axis runs over, the one named last changes fastest.
Arguments:
- residual: bfloat16 [512, 5120], P(('groups', 'ctx', 'row')), parts along dimension 0, may hold values from -6 to 6
- queries: bfloat16 [512, 20, 128], P('groups', 'head'), parts along dimension 0, may hold values from -160 to 160
- incoming_keys: bfloat16 [512, 4, 128], P(('groups', 'ctx', 'row'), 'head'), parts along dimension 0, may hold values from -6 to 6
- incoming_values: bfloat16 [512, 4, 128], P(('groups', 'ctx', 'row'), 'head'), parts along dimension 0, may hold values from -6 to 6
- cache_keys: bfloat16 [32768, 4, 128], P(('groups', 'ctx', 'row'), 'head'), parts along dimension 0, may hold values from -7 to 7
- cached_value_rows: bfloat16 [32768, 4, 128], P(('groups', 'ctx', 'row'), 'head'), parts along dimension 0, may hold values from -6 to 6
- context: int32 [2], P('groups'), parts along dimension 0, may hold values from 4096 to 16384
- attention_out: bfloat16 [2560, 5120], P('head', ('ctx', 'row')), may hold values from -1.5 to 1.5
- mixer_input: bfloat16 [512, 32, 128], P('groups', 'head', ('ctx', 'row')), parts along dimension 0, may hold values from -6 to 6
- mixer_gate: bfloat16 [512, 32, 128], P('groups', 'head', ('ctx', 'row')), parts along dimension 0, may hold values from -6 to 6
- state_in: bfloat16 [512, 256], P('groups'), parts along dimension 0, may hold values from -6 to 6
- state_out: bfloat16 [512, 256], P('groups'), parts along dimension 0, may hold values from -1.5 to 1.5
- step_size: float32 [512, 32], P('groups', 'head'), parts along dimension 0, may hold values from 0 to 2, as said below
- decay_log: float32 [32], P('head'), may hold values from -1 to 1
- skip_gain: float32 [32], P('head'), may hold values from 0.5 to 1.5
- prior_state: float32 [64, 128, 256], P(('groups', 'head'), ('ctx', 'row')), parts along dimension 0, may hold values from -1.5 to 1.5
- mixer_out: bfloat16 [4096, 5120], P('head', ('ctx', 'row')), may hold values from -0.09375 to 0.09375
- norm_gain: float32 [5120], replicated, may hold values from 0.5 to 1.5
- hidden_gate: bfloat16 [5120, 21504], P('head', ('ctx', 'row')), may hold values from -0.078125 to 0.078125
- hidden_up: bfloat16 [5120, 21504], P('head', ('ctx', 'row')), may hold values from -0.078125 to 0.078125
- hidden_down: bfloat16 [21504, 5120], P(('ctx', 'row'), 'head'), may hold values from -0.0390625 to 0.0390625
Outputs:
- block_out: bfloat16 [512, 5120], P(('groups', 'ctx', 'row'), 'head'), parts along dimension 0
There are 2 independent parts, one for each index of `groups`. A program takes and returns all parts, laid end to end along the dimension named above; an argument that names none is the same for every part. Nothing has to cross between parts.
Inputs may be any that keep to these rules, and one draw needn't show every extreme that they name: The cached slots below context are valid; the new tokens follow them. `step_size`: positive.
All inputs are finite; a program needn't handle non-finite values.
Results may differ from a plain program's by a relative error of at most 0.01.
Values may be sent and summed in bfloat16 or wider, within the bound.
No kernel may reach another device: no remote copies, remote signals or barrier semaphores. Data moves between devices by JAX's collectives and lax.ppermute only.
A program may use at most 128 MiB of HBM per device.

v0:
```python
import math

import jax
import jax.numpy as jnp
from jax import lax
from jax.sharding import PartitionSpec as P

very_low = -1e30


def combined_all(part, axis, combine):
    gathered = jax.tree.map(lambda a: lax.all_gather(a, axis), part)

    def take(source):
        return jax.tree.map(lambda a: lax.dynamic_index_in_dim(a, source, 0, False), gathered)

    return lax.fori_loop(
        1, lax.axis_size(axis), lambda source, state: combine(state, take(source)), take(0)
    )


def absorb(partial_state, scores, visible, block_values):
    running_sum, weight_total, running_peak = partial_state
    masked = jnp.where(visible, scores, very_low)
    top_score = jnp.maximum(running_peak, jnp.max(masked, axis=3))
    weights = jnp.where(visible, jnp.exp(masked - top_score[..., None]), 0.0)
    fade_factor = jnp.exp(running_peak - top_score)
    mixed_values = jnp.einsum(
        "kgts,skd->kgtd",
        weights.astype(jnp.bfloat16),
        block_values,
        preferred_element_type=jnp.float32,
    )
    return (
        running_sum * fade_factor[..., None] + mixed_values,
        weight_total * fade_factor + jnp.sum(weights, axis=3),
        top_score,
    )


def join_partial(first, second):
    sum_first, total_first, peak_first = first
    sum_second, total_second, peak_second = second
    common = jnp.maximum(peak_first, peak_second)
    fade_first = jnp.exp(peak_first - common)
    fade_second = jnp.exp(peak_second - common)
    return (
        sum_first * fade_first[..., None] + sum_second * fade_second[..., None],
        total_first * fade_first + total_second * fade_second,
        common,
    )


def scan_mixer(
    mixer_input, mixer_gate, state_in, state_out, step_size, decay_log, skip_gain, prior_state
):
    tokens = mixer_input.shape[0]
    decay_rate = -jnp.exp(decay_log)
    log_fade = jnp.cumsum(step_size * decay_rate[None, :], axis=0)
    token_order = jnp.arange(tokens)
    causal_mask = token_order[:, None] >= token_order[None, :]
    fade_heads = jnp.transpose(log_fade)
    differ = fade_heads[:, :, None] - fade_heads[:, None, :]
    lower_fade = jnp.exp(jnp.where(causal_mask[None], differ, very_low))
    state_match = jnp.einsum("tn,sn->ts", state_out, state_in, preferred_element_type=jnp.float32)
    mixing = lower_fade * state_match[None]
    inputs_wide = mixer_input.astype(jnp.float32)
    scaled = step_size[:, :, None] * inputs_wide
    inner_part = jnp.einsum("hts,shp->thp", mixing, scaled, precision=lax.Precision.HIGHEST)
    carried = (
        jnp.einsum(
            "tn,hpn->thp",
            state_out.astype(jnp.float32),
            prior_state,
            precision=lax.Precision.HIGHEST,
        )
        * jnp.exp(log_fade)[:, :, None]
    )
    mixed_out = inner_part + carried + skip_gain[None, :, None] * inputs_wide
    return (mixed_out * jax.nn.silu(mixer_gate.astype(jnp.float32))).astype(jnp.bfloat16)


def on_device(
    residual,
    queries,
    incoming_keys,
    incoming_values,
    cache_keys,
    cached_value_rows,
    context,
    attention_out,
    mixer_input,
    mixer_gate,
    state_in,
    state_out,
    step_size,
    decay_log,
    skip_gain,
    prior_state,
    mixer_out,
    norm_gain,
    hidden_gate,
    hidden_up,
    hidden_down,
):
    tokens = queries.shape[0]
    head_depth = queries.shape[2]
    shared_heads = cache_keys.shape[1]
    group_width = queries.shape[1] // shared_heads
    local_span = cache_keys.shape[0]
    fresh_count = incoming_keys.shape[0]
    owner_index = lax.axis_index(("ctx", "row"))
    score_scale = 1.0 / math.sqrt(head_depth)
    query_view = queries.reshape(tokens, shared_heads, group_width, head_depth)
    block_size = min(512, local_span)
    blocks = local_span // block_size
    key_blocks = cache_keys.reshape(blocks, block_size, shared_heads, head_depth)
    value_blocks = cached_value_rows.reshape(blocks, block_size, shared_heads, head_depth)

    def visit_block(partial_state, inputs):
        block_keys, block_values, block_number = inputs
        scores = (
            jnp.einsum("tkgd,skd->kgts", query_view, block_keys, preferred_element_type=jnp.float32)
            * score_scale
        )
        position = owner_index * local_span + block_number * block_size + jnp.arange(block_size)
        visible = (position < context[0])[None, None, None, :]
        return (absorb(partial_state, scores, visible, block_values), None)

    start_state = (
        jnp.zeros((shared_heads, group_width, tokens, head_depth), jnp.float32),
        jnp.zeros((shared_heads, group_width, tokens), jnp.float32),
        jnp.full((shared_heads, group_width, tokens), very_low, jnp.float32),
    )
    partial_state = lax.scan(
        visit_block, start_state, (key_blocks, value_blocks, jnp.arange(blocks))
    )[0]
    fresh_scores = (
        jnp.einsum("tkgd,skd->kgts", query_view, incoming_keys, preferred_element_type=jnp.float32)
        * score_scale
    )
    source = owner_index * fresh_count + jnp.arange(fresh_count)
    fresh_visible = (source[None, :] <= jnp.arange(tokens)[:, None])[None, None]
    running_sum, weight_total, running_peak = absorb(
        partial_state, fresh_scores, fresh_visible, incoming_values
    )
    merged = combined_all((running_sum, weight_total, running_peak), ("ctx", "row"), join_partial)
    attended = (merged[0] / merged[1][..., None]).astype(jnp.bfloat16)
    attention_part = jnp.einsum(
        "kgtd,kgdc->tc",
        attended,
        attention_out.reshape(shared_heads, group_width, head_depth, -1),
        preferred_element_type=jnp.float32,
    )
    gated = scan_mixer(
        mixer_input, mixer_gate, state_in, state_out, step_size, decay_log, skip_gain, prior_state
    )
    mixer_rows = mixer_out.reshape(mixer_input.shape[1], -1, mixer_out.shape[1])
    mixer_part = jnp.einsum(
        "thp,hpc->tc",
        lax.all_gather(gated, ("ctx", "row"), axis=2, tiled=True),
        mixer_rows,
        preferred_element_type=jnp.float32,
    )
    branches = attention_part + mixer_part
    summed = lax.psum(branches, "head")
    combined = lax.all_to_all(summed, ("ctx", "row"), split_axis=0, concat_axis=1, tiled=True)
    trunk = (residual.astype(jnp.float32) + combined).astype(jnp.bfloat16)
    trunk_wide = trunk.astype(jnp.float32)
    inverse_rms = lax.rsqrt(jnp.mean(trunk_wide * trunk_wide, axis=1, keepdims=True) + 1e-05)
    normed = (trunk_wide * inverse_rms * norm_gain[None, :]).astype(jnp.bfloat16)
    column_count = hidden_gate.shape[0]
    column_start = lax.axis_index("head") * column_count
    normed_part = lax.dynamic_slice_in_dim(normed, column_start, column_count, 1)
    segment = lax.all_gather(normed_part, ("ctx", "row"), axis=0, tiled=True)
    pair_partial = jnp.stack(
        [
            jnp.dot(segment, hidden_gate, preferred_element_type=jnp.float32),
            jnp.dot(segment, hidden_up, preferred_element_type=jnp.float32),
        ]
    )
    pair_share = lax.psum_scatter(pair_partial, "head", scatter_dimension=1, tiled=True)
    hidden_share = (jax.nn.silu(pair_share[0]) * pair_share[1]).astype(jnp.bfloat16)
    hidden = lax.all_gather(hidden_share, "head", axis=0, tiled=True)
    down_rows = lax.psum_scatter(
        jnp.dot(hidden, hidden_down, preferred_element_type=jnp.float32),
        ("ctx", "row"),
        scatter_dimension=0,
        tiled=True,
    )
    trunk_part = lax.dynamic_slice_in_dim(trunk_wide, column_start, column_count, 1)
    return (trunk_part + down_rows).astype(jnp.bfloat16)


def solution(mesh):
    in_specs = (
        P(("groups", "ctx", "row"), None),
        P("groups", "head", None),
        P(("groups", "ctx", "row"), "head", None),
        P(("groups", "ctx", "row"), "head", None),
        P(("groups", "ctx", "row"), "head", None),
        P(("groups", "ctx", "row"), "head", None),
        P("groups"),
        P("head", ("ctx", "row")),
        P("groups", "head", ("ctx", "row")),
        P("groups", "head", ("ctx", "row")),
        P("groups", None),
        P("groups", None),
        P("groups", "head"),
        P("head"),
        P("head"),
        P(("groups", "head"), ("ctx", "row"), None),
        P("head", ("ctx", "row")),
        P(),
        P("head", ("ctx", "row")),
        P("head", ("ctx", "row")),
        P(("ctx", "row"), "head"),
    )
    out_specs = P(("groups", "ctx", "row"), "head")
    return jax.shard_map(
        on_device, mesh=mesh, in_specs=in_specs, out_specs=out_specs, check_vma=False
    )
```

profile of v0, /device:TPU:0, one launch (start us, length us, event | category | flops | bytes accessed | tf_op | source)
XLA Modules:
  0.0 461.4 jit_solution(2985679149651209535)
XLA Ops:
  10.4 5.1 %fusion.43 = f32[256,16,16]{0,2,1:T(8,128)S(1)} fusion(f32[256,256]{1,0:T(8,128)S(1)} %fusion.68, f32[16,256]{1,0:T(8,128)S(1)} %copy_bitcast_fusion.4, pred[256,256]{1,0:T(8,128)(4,1)S(1)} %iota_compare_fusion, bf16[256,16,16]{0,2,1:T(8,128)(2,1)} %param.33, f32[256,16]{0,1:T(8,128)} %param.37), kind=kOutput, calls=%fused_computation.63 | convolution fusion | flops 204603392 | bytes 753664 | tf_op jit(solution)/shard_map/hts,shp->thp/dot_general | solution.py:69
  17.1 67.7 %while.37 = (s32[]{:T(128)}, f32[2,5,256,128]{3,2,1,0:T(8,128)}, f32[2,5,256]{2,1,0:T(8,128)}, f32[2,5,256]{2,1,0:T(8,128)S(1)}, s32[4]{0:T(128)}, /*index=5*/s3...) while((s32[]{:T(128)}, f32[2,5,256,128]{3,2,1,0:T(8,128)}, ...), condition=%wide.region_3.4_spmd.clone, body=%wide.region_0.3_spmd.clone.sunk | while | flops 689124864 | bytes 41802048 | solution.py:135
  21.1 3.8 bitcast_reduce_fusion.2
  25.6 3.7 fusion.94
  37.0 3.8 bitcast_reduce_fusion.2
  45.9 4.5 fusion.96
  54.3 3.8 bitcast_reduce_fusion.2
  63.1 4.5 fusion.96
  71.5 3.8 bitcast_reduce_fusion.2
  80.3 4.5 fusion.96
  89.9 15.7 %all-gather.1 = f32[16,5,256]{2,1,0:T(8,128)S(1)} all-gather(f32[2,5,256]{2,1,0:T(8,128)S(1)} %get-tuple-element.400), channel_id=3, replica_groups=mesh['groups'=2,'ctx'=4,'head'=2,'row'=2] {'ctx','row'}, dimensions={0}, use_global_device_ids=true | all-gather | bytes 92160 | tf_op jit(solution)/shard_map/all_gather | solution.py:12
  105.6 16.6 %all-gather.2 = f32[16,5,256]{2,1,0:T(8,128)S(1)} all-gather(f32[2,5,256]{2,1,0:T(8,128)S(1)} %max.18), channel_id=4, replica_groups=mesh['groups'=2,'ctx'=4,'head'=2,'row'=2] {'ctx','row'}, dimensions={0}, use_global_device_ids=true | all-gather | bytes 92160 | tf_op jit(solution)/shard_map/all_gather | solution.py:12
  125.3 67.8 %all-gather.14.cloned.1.call-done = f32[16,5,256,128]{3,2,1,0:T(8,128)} async-done(((f32[2,5,256,128]{3,2,1,0:T(8,128)}), f32[16,5,256,128]{3,2,1,0:T(8,128)}) %all-gather.14.cloned.1.call-update) | async-done | bytes 10485776 | tf_op jit(solution)/shard_map/all_gather | solution.py:12
  194.5 14.7 %while.36 = (s32[]{:T(128)}, f32[2,5,256,128]{3,2,1,0:T(8,128)S(1)}, f32[2,5,256]{2,1,0:T(8,128)S(1)}, f32[2,5,256]{2,1,0:T(8,128)S(1)}, f32[8,2,5,256]{3,2,1,0:...) while((s32[]{:T(128)}, ...), condition=%wide.region_7.8_spmd, body=%wide.region_6.7_spmd.sunk | while | flops 998405 | bytes 4034711 | solution.py:17
  212.3 30.0 %all-reduce.2.cloned.1.call-done = f32[8,32,640]{2,1,0:T(8,128)} async-done(((f32[8,32,640]{2,1,0:T(8,128)}), f32[8,32,640]{2,1,0:T(8,128)}) %all-reduce.2.cloned.1.call-update) | async-done | bytes 655376 | tf_op jit(solution)/shard_map/psum | solution.py:166
  242.3 4.6 all-to-all-start
  247.0 18.0 %all-to-all-done = f32[8,32,640]{2,1,0:T(8,128)S(1)} async-done(((f32[8,32,640]{2,1,0:T(8,128)}), f32[8,32,640]{2,1,0:T(8,128)S(1)}, u32[]{:S(2)}, u32[]{:S(2)}) %all-to-all-start) | async-done | bytes 655392 | tf_op jit(solution)/shard_map/all_to_all | solution.py:167
  266.1 21.5 %all-gather.10.cloned.1.call-done = bf16[256,2560]{1,0:T(8,128)(2,1)} async-done(((bf16[32,2560]{1,0:T(8,128)(2,1)}), bf16[256,2560]{1,0:T(8,128)(2,1)}) %all-gather.10.cloned.1.call-update) | async-done | bytes 1310736 | tf_op jit(solution)/shard_map/all_gather | solution.py:175
  287.6 9.7 %convolution_bitcast_fusion = f32[1,256,2688]{2,1,0:T(8,128)S(1)} fusion(bf16[256,2560]{1,0:T(8,128)(2,1)} %all-gather.10.cloned.1.call-done, bf16[2560,2688]{1,0:T(8,128)(2,1)} %param.44), kind=kOutput, calls=%fused_computation.39 | convolution fusion | flops 3523215360 | bytes 17825792 | tf_op jit(solution)/shard_map/dot_general | solution.py:179
  297.3 7.5 %convolution_bitcast_fusion.1 = f32[1,256,2688]{2,1,0:T(8,128)S(1)} fusion(bf16[256,2560]{1,0:T(8,128)(2,1)S(1)} %copy-done.11, bf16[2560,2688]{1,0:T(8,128)(2,1)} %param.43), kind=kOutput, calls=%fused_computation.40 | convolution fusion | flops 3523215360 | bytes 17825792 | tf_op jit(solution)/shard_map/dot_general | solution.py:178
  307.7 68.2 %reduce-scatter.3.cloned.1.call-done = f32[2,128,2688]{2,1,0:T(8,128)} async-done(((f32[2,256,2688]{2,1,0:T(8,128)}), f32[2,128,2688]{2,1,0:T(8,128)}) %reduce-scatter.3.cloned.1.call-update) | async-done | bytes 2752528 | tf_op jit(solution)/shard_map/reduce_scatter | solution.py:182
  379.0 25.1 %all-gather.12.cloned.1.call-done = bf16[256,2688]{1,0:T(8,128)(2,1)} async-done(((bf16[128,2688]{1,0:T(8,128)(2,1)}), bf16[256,2688]{1,0:T(8,128)(2,1)}) %all-gather.12.cloned.1.call-update) | async-done | bytes 1376272 | tf_op jit(solution)/shard_map/all_gather | solution.py:184
  404.1 10.8 %fusion.69 = f32[256,2560]{1,0:T(8,128)} fusion(bf16[256,2688]{1,0:T(8,128)(2,1)} %all-gather.12.cloned.1.call-done, bf16[2688,2560]{1,0:T(8,128)(2,1)} %param.45), kind=kOutput, calls=%fused_computation.106 | convolution fusion | flops 3523215360 | bytes 17760256 | tf_op jit(solution)/shard_map/dot_general | solution.py:186
  414.9 38.0 %reduce-scatter.5.cloned.1.call-done = f32[32,2560]{1,0:T(8,128)} async-done(((f32[256,2560]{1,0:T(8,128)}), f32[32,2560]{1,0:T(8,128)}) %reduce-scatter.5.cloned.1.call-update) | async-done | bytes 327696 | tf_op jit(solution)/shard_map/reduce_scatter | solution.py:185
  (156 shorter events, 74.0 us)
Async XLA Ops:
  6.5 115.7 %copy-start = (bf16[2048,640]{1,0:T(8,128)(2,1)S(1)}, bf16[2048,640]{1,0:T(8,128)(2,1)}, u32[]{:S(2)}) copy-start(bf16[2048,640]{1,0:T(8,128)(2,1)} %param.41) | copy-start | bytes 7864324
  6.5 115.7 %all-gather.8.cloned.1.call-start = ((), (), s32[]{:S(2)}) async-start(), calls=%async_computation.3 | async-start | bytes 1179648 | tf_op jit(solution)/shard_map/all_gather | solution.py:161
  10.3 5.1 %copy-start.9 = (bf16[256,256]{1,0:T(8,128)(2,1)S(1)}, bf16[256,256]{1,0:T(8,128)(2,1)}, u32[]{:S(2)}) copy-start(bf16[256,256]{1,0:T(8,128)(2,1)} %param.36) | copy-start | bytes 393220
  10.3 5.1 %copy-start.12 = (f32[16,16,256]{2,1,0:T(8,128)S(1)}, f32[16,16,256]{2,1,0:T(8,128)}, u32[]{:S(2)}) copy-start(f32[16,16,256]{2,1,0:T(8,128)} %param.40) | copy-start | bytes 786436
  10.3 5.1 %copy-start.13 = (bf16[256,16,16]{0,2,1:T(8,128)(2,1)S(1)}, bf16[256,16,16]{0,2,1:T(8,128)(2,1)}, u32[]{:S(2)}) copy-start(bf16[256,16,16]{0,2,1:T(8,128)(2,1)} %param.33) | copy-start | bytes 393220
  10.3 5.1 %copy-start.14 = (bf16[256,16,16]{0,2,1:T(8,128)(2,1)S(1)}, bf16[256,16,16]{0,2,1:T(8,128)(2,1)}, u32[]{:S(2)}) copy-start(bf16[256,16,16]{0,2,1:T(8,128)(2,1)} %param.34) | copy-start | bytes 393220
  10.3 5.1 %copy-start.15 = (f32[16]{0:T(128)S(1)}, f32[16]{0:T(128)}, u32[]{:S(2)}) copy-start(f32[16]{0:T(128)} %param.39) | copy-start | bytes 196
  10.4 6.8 %copy-start.3 = (bf16[256,10,128]{2,0,1:T(8,128)(2,1)S(1)}, bf16[256,10,128]{2,0,1:T(8,128)(2,1)}, u32[]{:S(2)}) copy-start(bf16[256,10,128]{2,0,1:T(8,128)(2,1)} %param.26) | copy-start | bytes 1966084
  16.5 176.6 %all-gather.14.cloned.1.call-start = ((), (), s32[]{:S(2)}) async-start(), calls=%async_computation.9 | async-start | bytes 11796480 | tf_op jit(solution)/shard_map/all_gather | solution.py:12
  19.7 5.2 %copy-start.7 = (pred[512]{0:T(512)(128)(4,1)}, pred[512]{0:T(512)(128)(4,1)S(1)}, u32[]{:S(2)}) copy-start(pred[512]{0:T(512)(128)(4,1)S(1)} %add_compare_fusion.2) | copy-start | bytes 1540 | tf_op jit(solution)/shard_map/while
  35.6 5.2 %copy-start.7 = (pred[512]{0:T(512)(128)(4,1)}, pred[512]{0:T(512)(128)(4,1)S(1)}, u32[]{:S(2)}) copy-start(pred[512]{0:T(512)(128)(4,1)S(1)} %add_compare_fusion.2) | copy-start | bytes 1540 | tf_op jit(solution)/shard_map/while
  52.9 5.2 %copy-start.7 = (pred[512]{0:T(512)(128)(4,1)}, pred[512]{0:T(512)(128)(4,1)S(1)}, u32[]{:S(2)}) copy-start(pred[512]{0:T(512)(128)(4,1)S(1)} %add_compare_fusion.2) | copy-start | bytes 1540 | tf_op jit(solution)/shard_map/while
  70.1 5.2 %copy-start.7 = (pred[512]{0:T(512)(128)(4,1)}, pred[512]{0:T(512)(128)(4,1)S(1)}, u32[]{:S(2)}) copy-start(pred[512]{0:T(512)(128)(4,1)S(1)} %add_compare_fusion.2) | copy-start | bytes 1540 | tf_op jit(solution)/shard_map/while
  89.8 152.5 %all-reduce.2.cloned.1.call-start = ((), (), s32[]{:S(2)}) async-start(), calls=%async_computation.4 | async-start | bytes 1310720 | tf_op jit(solution)/shard_map/psum | solution.py:166
  194.5 14.7 %copy-start.16 = (f32[256,640]{1,0:T(8,128)S(1)}, f32[256,640]{1,0:T(8,128)}, u32[]{:S(2)}) copy-start(f32[256,640]{1,0:T(8,128)} %convolution_bitcast_fusion.2) | copy-start | bytes 1966084
  209.2 37.7 %copy-start.10 = (f32[5120]{0:T(1024)S(1)}, f32[5120]{0:T(1024)}, u32[]{:S(2)}) copy-start(f32[5120]{0:T(1024)} %param.42) | copy-start | bytes 61444
  212.3 52.8 %copy-start.6 = (bf16[32,5120]{1,0:T(8,128)(2,1)S(1)}, bf16[32,5120]{1,0:T(8,128)(2,1)}, u32[]{:S(2)}) copy-start(bf16[32,5120]{1,0:T(8,128)(2,1)} %param.25) | copy-start | bytes 983044
  242.3 22.7 %all-to-all-start = ((f32[8,32,640]{2,1,0:T(8,128)}), f32[8,32,640]{2,1,0:T(8,128)S(1)}, u32[]{:S(2)}, u32[]{:S(2)}) async-start(f32[8,32,640]{2,1,0:T(8,128)} %all-reduce.2.cloned.1.call-done), calls=%async_computation | async-start | bytes 1310720 | tf_op jit(solution)/shard_map/all_to_all | solution.py:167
  246.9 40.7 %all-gather.10.cloned.1.call-start = ((), (), s32[]{:S(2)}) async-start(), calls=%async_computation.5 | async-start | bytes 1474560 | tf_op jit(solution)/shard_map/all_gather | solution.py:175
  266.1 109.8 %reduce-scatter.3.cloned.1.call-start = ((), (), s32[]{:S(2)}) async-start(), calls=%async_computation.6 | async-start | bytes 8257536 | tf_op jit(solution)/shard_map/reduce_scatter | solution.py:182
  287.6 9.7 %copy-start.11 = (bf16[256,2560]{1,0:T(8,128)(2,1)S(1)}, bf16[256,2560]{1,0:T(8,128)(2,1)}, u32[]{:S(2)}) copy-start(bf16[256,2560]{1,0:T(8,128)(2,1)} %all-gather.10.cloned.1.call-done) | copy-start | bytes 3932164
  307.6 96.4 %all-gather.12.cloned.1.call-start = ((), (), s32[]{:S(2)}) async-start(), calls=%async_computation.7 | async-start | bytes 2064384 | tf_op jit(solution)/shard_map/all_gather | solution.py:184
  378.9 74.0 %reduce-scatter.5.cloned.1.call-start = ((), (), s32[]{:S(2)}) async-start(), calls=%async_computation.8 | async-start | bytes 2949120 | tf_op jit(solution)/shard_map/reduce_scatter | solution.py:185
  404.1 50.5 %copy-start.1 = (bf16[2048,640]{1,0:T(8,128)(2,1)S(1)}, bf16[2048,640]{1,0:T(8,128)(2,1)}, u32[]{:S(2)}) copy-start(bf16[2048,640]{1,0:T(8,128)(2,1)} %param.41) | copy-start | bytes 7864324
  (16 other events, 51.7 us)
Sparse Core Ops, SparseCore 0:
  16.6 24.9 all-gather.7
  89.9 103.0 all-gather.13
  212.4 29.8 all-reduce.1
  266.2 21.3 all-gather.9
  307.7 68.1 reduce-scatter.2
  379.0 24.9 all-gather.11
  415.0 37.8 reduce-scatter.4
where the time goes:
time: 463 us; the launch traced here: 461 us
  waiting for transfers between devices  269 us (58%)
  matrix products  77.1 us (17%)
  other arithmetic  46.4 us (10%)
  blocking collectives  32.3 us (7%)
  local copies, waits for them, and re-layouts  15.3 us (3%)
  between operations  13.8 us (3%)
  starting transfers between devices  4.85 us (1%)
    reduce_scatter x1, waiting for transfers between devices, on_device(): lax.psum_scatter(pair_partial, 'head', scatter_dimension=1, tiled=True)  68.2 us
    all_gather x1, waiting for transfers between devices, combined_all(): gathered = jax.tree.map(lambda a: lax.all_gather(a, axis), part)  67.8 us
    reduce_scatter x1, waiting for transfers between devices, on_device(): lax.psum_scatter(jnp.dot(hidden, hidden_down, preferred_element_type=jnp....  38 us
    all_gather x2, blocking collectives, combined_all(): gathered = jax.tree.map(lambda a: lax.all_gather(a, axis), part)  32.3 us
    psum x1, waiting for transfers between devices, on_device(): summed = lax.psum(branches, 'head')  30 us
    all_gather x1, waiting for transfers between devices, on_device(): hidden = lax.all_gather(hidden_share, 'head', axis=0, tiled=True)  25.1 us
    all_gather x1, waiting for transfers between devices, on_device(): segment = lax.all_gather(normed_part, ('ctx', 'row'), axis=0, tiled=True)  21.5 us
    dot_general x5, matrix products, absorb(): jnp.einsum('kgts,skd->kgtd', weights.astype(jnp.bfloat16), block_values,...  19.5 us
  transfers between devices with their start and end apart: 8, of which 7 were waited for; matrix products, arithmetic and copies ran while one was open for 15% of the time, Pallas kernels for 0%

commit v1 on v0

--- a/solution.py
+++ b/solution.py
@@ -1,11 +1,18 @@
+import functools
 import math
 
 import jax
 import jax.numpy as jnp
 from jax import lax
+from jax.experimental import pallas as pl
+from jax.experimental.pallas import tpu as pltpu
 from jax.sharding import PartitionSpec as P
 
 very_low = -1e30
+lowest_peak = -1e20
+lanes = 128
+bf16 = jnp.bfloat16
+f32 = jnp.float32
 
 
 def combined_all(part, axis, combine):
@@ -80,7 +87,7 @@
     return (mixed_out * jax.nn.silu(mixer_gate.astype(jnp.float32))).astype(jnp.bfloat16)
 
 
-def on_device(
+def general_form(
     residual,
     queries,
     incoming_keys,
@@ -192,6 +199,544 @@
     return (trunk_part + down_rows).astype(jnp.bfloat16)
 
 
+smem = pl.BlockSpec(memory_space=pltpu.SMEM)
+whole = pl.BlockSpec(memory_space=pltpu.VMEM)
+
+
+def local_call(kernel, outs, *args, scratch=(), cost=None, name=None):
+    return pl.pallas_call(
+        kernel,
+        out_shape=tuple(jax.ShapeDtypeStruct(s, d) for s, d in outs),
+        in_specs=[smem] + [whole] * (len(args) - 1),
+        out_specs=tuple(whole for _ in outs),
+        scratch_shapes=list(scratch),
+        cost_estimate=cost,
+        name=name,
+    )(*args)
+
+
+def wrap(x, n):
+    return jnp.where(x >= n, x - n, x)
+
+
+def split_three(x):
+    high = x.astype(bf16).astype(f32)
+    rest = x - high
+    middle = rest.astype(bf16).astype(f32)
+    return high, middle, rest - middle
+
+
+def put_stats(table, head, peak, total):
+    lane = lax.broadcasted_iota(jnp.int32, table.shape, 1) - 6 * head
+    for i, piece in enumerate(split_three(peak) + split_three(total)):
+        table = jnp.where(lane == i, piece, table)
+    return table
+
+
+def get_stats(table, head):
+    at = 6 * head
+
+    def three(a):
+        return table[:, a : a + 1] + table[:, a + 1 : a + 2] + table[:, a + 2 : a + 3]
+
+    return three(at), three(at + 3)
+
+
+def attention_kernel(
+    dims, sc, q, k, v, fresh_k, fresh_v, keep, send, keys, values, stats
+):
+    nc, nr, kv, width, span, fresh, scale2 = dims
+    head = pl.program_id(0)
+    heads = kv * width
+    z, r, limit = sc[0], sc[1], sc[3]
+    rows = nc * nr * fresh
+
+    @pl.when(head == 0)
+    def _():
+        i = lax.broadcasted_iota(jnp.int32, (kv * lanes, kv * lanes), 0)
+        j = lax.broadcasted_iota(jnp.int32, (kv * lanes, kv * lanes), 1)
+        pick = ((i % lanes) * kv + i // lanes == j).astype(bf16)
+        for source, target in ((k, keys), (v, values)):
+            for b in range(span // lanes):
+                part = jnp.dot(
+                    pick, source[b * kv * lanes : (b + 1) * kv * lanes, :],
+                    preferred_element_type=f32,
+                ).astype(bf16)
+                for g in range(kv):
+                    target[g, b * lanes : (b + 1) * lanes, :] = part[g * lanes : (g + 1) * lanes]
+        for source, target in ((fresh_k, keys), (fresh_v, values)):
+            part = jnp.dot(
+                pick[:, : kv * fresh], source[...], preferred_element_type=f32
+            ).astype(bf16)
+            for g in range(kv):
+                target[g, span : span + lanes, :] = part[g * lanes : (g + 1) * lanes]
+        stats[...] = jnp.zeros_like(stats)
+
+    g = head // width
+    query = jnp.concatenate(
+        [q[0, wrap(z + a, nc) * nr + wrap(r + s, nr)] for s in range(nr) for a in range(nc)], axis=0
+    )
+    scores = lax.dot_general(
+        query, keys[g], (((1,), (1,)), ((), ())), preferred_element_type=f32
+    )
+    cached, new = scores[:, :span], scores[:, span:]
+    column = lax.broadcasted_iota(jnp.int32, (1, span), 1)
+    cached = jnp.where(column < limit, cached, very_low)
+    place = lax.broadcasted_iota(jnp.int32, (rows, lanes), 0)
+    n = lax.broadcasted_iota(jnp.int32, (rows, lanes), 1)
+    s, a, t = place // (nc * fresh), (place // fresh) % nc, place % fresh
+    token = (wrap(z + a, nc) * nr + wrap(r + s, nr)) * fresh + t
+    seen = (n < fresh) & ((z * nr + r) * fresh + n <= token)
+    new = jnp.where(seen, new, very_low)
+    peak = jnp.maximum(jnp.max(cached, axis=1, keepdims=True), jnp.max(new, axis=1, keepdims=True))
+    peak = jnp.maximum(peak, lowest_peak)
+    weights = jnp.exp2((cached - peak) * scale2)
+    weights_new = jnp.exp2((new - peak) * scale2)
+    total = jnp.sum(weights, axis=1, keepdims=True) + jnp.sum(weights_new, axis=1, keepdims=True)
+    mixed = jnp.dot(weights.astype(bf16), values[g, :span, :], preferred_element_type=f32)
+    mixed += jnp.dot(weights_new.astype(bf16), values[g, span:, :], preferred_element_type=f32)
+    half = nc * fresh
+    at = pl.multiple_of(head * lanes, lanes)
+    mixed = mixed.astype(bf16)
+    keep[:, pl.ds(at, lanes)] = mixed[:half]
+    send[:, pl.ds(at, lanes)] = mixed[half:]
+    stats[...] = put_stats(stats[...], head, peak * scale2, total)
+
+    @pl.when(head == heads - 1)
+    def _():
+        keep[:, heads * lanes :] = stats[:half].astype(bf16)
+        send[:, heads * lanes :] = stats[half:].astype(bf16)
+
+
+def merge_parts(heads, parts, finish):
+    tables = [p[:, heads * lanes :].astype(f32) for p in parts]
+    for h in range(heads):
+        stats = [get_stats(t, h) for t in tables]
+        peak = functools.reduce(jnp.maximum, [m for m, _ in stats])
+        fades = [jnp.exp2(m - peak) for m, _ in stats]
+        mixed = sum(
+            p[:, h * lanes : (h + 1) * lanes].astype(f32) * f for p, f in zip(parts, fades)
+        )
+        total = sum(l * f for (_, l), f in zip(stats, fades))
+        finish(h, mixed, peak, total)
+
+
+def merge_rows_kernel(dims, sc, mine, other, *outs):
+    heads, nc, fresh = dims
+    table = [jnp.zeros((nc * fresh, lanes), f32)]
+
+    def finish(h, mixed, peak, total):
+        mixed = mixed.astype(bf16)
+        for a, out in enumerate(outs):
+            out[:, h * lanes : (h + 1) * lanes] = mixed[a * fresh : (a + 1) * fresh]
+        table[0] = put_stats(table[0], h, peak, total)
+
+    merge_parts(heads, (mine, other), finish)
+    packed = table[0].astype(bf16)
+    for a, out in enumerate(outs):
+        out[:, heads * lanes :] = packed[a * fresh : (a + 1) * fresh]
+
+
+def merge_final_kernel(heads, sc, *refs):
+    parts, out = refs[:-1], refs[-1]
+
+    def finish(h, mixed, peak, total):
+        out[:, h * lanes : (h + 1) * lanes] = (mixed / total).astype(bf16)
+
+    merge_parts(heads, parts, finish)
+
+
+def mixer_project_kernel(dims, sc, mine, other, weight, out, full):
+    nc, nr, heads, channels = dims
+    z, r = sc[0], sc[1]
+    for s, source in enumerate((mine, other)):
+        for a in range(nc):
+            owner = wrap(z + a, nc) * nr + wrap(r + s, nr)
+            for h in range(heads):
+                at = pl.multiple_of(h * nc * nr * channels + owner * channels, channels)
+                full[pl.ds(at, channels), :] = source[a, h * channels : (h + 1) * channels, :]
+    out[...] = lax.dot_general(
+        full[...], weight[...], (((0,), (0,)), ((), ())), preferred_element_type=f32
+    )
+
+
+def branch_kernel(dims, sc, mine, other, weight, mixer_part, keep, send):
+    nc, nr, fresh = dims
+    z, r = sc[0], sc[1]
+    for s, (source, out) in enumerate(((mine, keep), (other, send))):
+        attention = jnp.dot(source[...], weight[...], preferred_element_type=f32)
+        for a in range(nc):
+            block = wrap(z + a, nc) * nr + wrap(r + s, nr)
+            at = pl.multiple_of(block * fresh, fresh)
+            rows = attention[a * fresh : (a + 1) * fresh] + mixer_part[pl.ds(at, fresh), :]
+            out[a * fresh : (a + 1) * fresh, :] = rows.astype(bf16)
+
+
+def side_by_side_kernel(dims, sc, mine, other, *outs):
+    fresh, columns = dims
+    r = sc[1]
+    for s, source in enumerate((mine, other)):
+        at = pl.multiple_of(wrap(r + s, 2) * columns, lanes)
+        for a, out in enumerate(outs):
+            out[:, pl.ds(at, columns)] = source[a * fresh : (a + 1) * fresh, :]
+
+
+def columns_kernel(dims, sc, *refs):
+    nc, columns = dims
+    z = sc[0]
+    out = refs[-1]
+    for a in range(nc):
+        at = pl.multiple_of(wrap(z + nc - a, nc) * columns, lanes)
+        out[:, pl.ds(at, columns)] = refs[a][...]
+
+
+def trunk_kernel(columns, sc, residual, mine, other, gain, normed_part, trunk_part, normed, trunk):
+    h = sc[2]
+    total = residual[...].astype(f32) + (mine[...].astype(f32) + other[...].astype(f32))
+    rounded = total.astype(bf16)
+    trunk[...] = rounded
+    wide = rounded.astype(f32)
+    inverse = lax.rsqrt(jnp.mean(wide * wide, axis=1, keepdims=True) + 1e-05)
+    normed[...] = (wide * inverse * gain[...]).astype(bf16)
+    at = pl.multiple_of(h * columns, lanes)
+    normed_part[...] = normed[:, pl.ds(at, columns)]
+    trunk_part[...] = trunk[:, pl.ds(at, columns)]
+
+
+def gate_up_kernel(unit, sc, mine, other, gate, up, keep, send, tokens):
+    h = sc[2]
+    half = mine.shape[0]
+
+    @pl.when((pl.program_id(0) == 0) & (h == 0))
+    def _():
+        tokens[:half, :] = mine[...]
+        tokens[half:, :] = other[...]
+
+    @pl.when((pl.program_id(0) == 0) & (h != 0))
+    def _():
+        tokens[:half, :] = other[...]
+        tokens[half:, :] = mine[...]
+
+    for i, weight in enumerate((gate, up)):
+        sums = jnp.dot(tokens[...], weight[...], preferred_element_type=f32)
+        keep[i] = sums[:half]
+        send[i] = sums[half:].astype(bf16)
+
+
+def gate_up(sc, mine, other, gate, up, start, width, unit):
+    half, depth = mine.shape
+    first = start // unit
+    steps = width // unit
+    table = pl.BlockSpec((half, depth), lambda j: (0, 0))
+    weight = pl.BlockSpec((depth, unit), lambda j: (0, first + j))
+    out = pl.BlockSpec((2, half, unit), lambda j: (0, 0, j))
+    return pl.pallas_call(
+        functools.partial(gate_up_kernel, unit),
+        grid=(steps,),
+        out_shape=(
+            jax.ShapeDtypeStruct((2, half, width), f32),
+            jax.ShapeDtypeStruct((2, half, width), bf16),
+        ),
+        in_specs=[smem, table, table, weight, weight],
+        out_specs=(out, out),
+        scratch_shapes=[pltpu.VMEM((2 * half, depth), bf16)],
+        cost_estimate=pl.CostEstimate(
+            flops=8 * half * depth * width, transcendentals=0, bytes_accessed=4 * depth * width
+        ),
+        name="gate_up",
+    )(sc, mine, other, gate, up)
+
+
+def hidden_kernel(sc, mine, other, out):
+    gate = mine[0] + other[0].astype(f32)
+    up = mine[1] + other[1].astype(f32)
+    out[...] = (gate / (1.0 + jnp.exp(-gate)) * up).astype(bf16)
+
+
+def down_kernel(widths, first, last, sc, *refs):
+    n = len(widths)
+    mine, other, weight = refs[:n], refs[n : 2 * n], refs[2 * n]
+    rest = refs[2 * n + 1 :]
+    hidden = rest[-1]
+    half = mine[0].shape[0]
+
+    @pl.when(pl.program_id(0) == 0)
+    def _():
+        at = 0
+        for m, o, w in zip(mine, other, widths):
+            hidden[:half, at : at + w] = m[...]
+            hidden[half:, at : at + w] = o[...]
+            at += w
+
+    sums = jnp.dot(hidden[...], weight[...], preferred_element_type=f32)
+    if not first:
+        sums += rest[0][...]
+    if not last:
+        rest[-2][...] = sums
+        return
+    keep, send = rest[-3], rest[-2]
+    h = sc[2]
+
+    @pl.when(h == 0)
+    def _():
+        keep[...] = sums[:half]
+        send[...] = sums[half:].astype(bf16)
+
+    @pl.when(h != 0)
+    def _():
+        keep[...] = sums[half:]
+        send[...] = sums[:half].astype(bf16)
+
+
+def down(sc, mine, other, weight, start, before, last):
+    half = mine[0].shape[0]
+    widths = tuple(m.shape[1] for m in mine)
+    depth = sum(widths)
+    columns = weight.shape[1]
+    unit = 512 if columns % 512 == 0 else columns
+    first = before is None
+    hid = [pl.BlockSpec((half, w), lambda j: (0, 0)) for w in widths]
+    both = pl.BlockSpec((2 * half, unit), lambda j: (0, j))
+    one = pl.BlockSpec((half, unit), lambda j: (0, j))
+    block = start // depth
+    outs = (
+        (jax.ShapeDtypeStruct((half, columns), f32), jax.ShapeDtypeStruct((half, columns), bf16))
+        if last
+        else jax.ShapeDtypeStruct((2 * half, columns), f32)
+    )
+    return pl.pallas_call(
+        functools.partial(down_kernel, widths, first, last),
+        grid=(columns // unit,),
+        out_shape=outs,
+        in_specs=[smem]
+        + hid
+        + hid
+        + [pl.BlockSpec((depth, unit), lambda j: (block, j))]
+        + ([] if first else [both]),
+        out_specs=(one, one) if last else both,
+        scratch_shapes=[pltpu.VMEM((2 * half, depth), bf16)],
+        cost_estimate=pl.CostEstimate(
+            flops=4 * half * depth * columns,
+            transcendentals=0,
+            bytes_accessed=2 * depth * columns + (0 if first else 8 * half * columns),
+        ),
+        name="down",
+    )(sc, *mine, *other, weight, *([] if first else [before]))
+
+
+def spread_kernel(fresh, sc, mine, other, own, *outs):
+    own[...] = mine[:fresh] + other[:fresh].astype(f32)
+    for a, out in enumerate(outs):
+        rows = slice((a + 1) * fresh, (a + 2) * fresh)
+        out[...] = (mine[rows] + other[rows].astype(f32)).astype(bf16)
+
+
+def finish_kernel(sc, trunk, own, *refs):
+    total = own[...]
+    for part in refs[:-1]:
+        total += part[...].astype(f32)
+    refs[-1][...] = (trunk[...].astype(f32) + total).astype(bf16)
+
+
+def small_form(
+    nc,
+    nr,
+    nh,
+    residual,
+    queries,
+    incoming_keys,
+    incoming_values,
+    cache_keys,
+    cached_value_rows,
+    context,
+    attention_out,
+    mixer_input,
+    mixer_gate,
+    state_in,
+    state_out,
+    step_size,
+    decay_log,
+    skip_gain,
+    prior_state,
+    mixer_out,
+    norm_gain,
+    hidden_gate,
+    hidden_up,
+    hidden_down,
+):
+    tokens, heads, depth = queries.shape
+    span, kv = cache_keys.shape[:2]
+    fresh = incoming_keys.shape[0]
+    half = nc * fresh
+    width = heads // kv
+    z, r, h = lax.axis_index("ctx"), lax.axis_index("row"), lax.axis_index("head")
+    limit = context[0] - (z * nr + r) * span
+    sc = jnp.stack([z, r, h, limit]).astype(jnp.int32)
+
+    def shift(x, by):
+        return lax.ppermute(x, "ctx", [(i, (i + by) % nc) for i in range(nc)])
+
+    def to_owners(parts):
+        return [parts[0]] + [shift(parts[a], a) for a in range(1, nc)]
+
+    def from_all(x):
+        return [x] + [shift(x, -a) for a in range(1, nc)]
+
+    def other_row(x):
+        return lax.ppermute(x, "row", [(i, (i + 1) % nr) for i in range(nr)])
+
+    def other_head(x):
+        return lax.ppermute(x, "head", [(i, (i + 1) % nh) for i in range(nh)])
+
+    gated = scan_mixer(
+        mixer_input, mixer_gate, state_in, state_out, step_size, decay_log, skip_gain, prior_state
+    )
+    state_heads, channels = gated.shape[1:]
+    gated = jnp.transpose(gated, (1, 2, 0)).reshape(state_heads * channels, tokens)
+    gated_all = jnp.stack(from_all(gated))
+    gated_other = other_row(gated_all)
+
+    dims = (nc, nr, kv, width, span, fresh, math.log2(math.e) / math.sqrt(depth))
+    wide = (heads + 1) * lanes
+    query_view = jnp.transpose(queries, (1, 0, 2)).reshape(heads, nc * nr, fresh, depth)
+    fixed = lambda shape: pl.BlockSpec(shape, lambda i: (0,) * len(shape))
+    keep, send = pl.pallas_call(
+        functools.partial(attention_kernel, dims),
+        grid=(heads,),
+        out_shape=(jax.ShapeDtypeStruct((half, wide), bf16),) * 2,
+        in_specs=[
+            smem,
+            pl.BlockSpec((1, nc * nr, fresh, depth), lambda i: (i, 0, 0, 0)),
+            fixed((span * kv, depth)),
+            fixed((span * kv, depth)),
+            fixed((fresh * kv, depth)),
+            fixed((fresh * kv, depth)),
+        ],
+        out_specs=(fixed((half, wide)),) * 2,
+        scratch_shapes=[
+            pltpu.VMEM((kv, span + lanes, depth), bf16),
+            pltpu.VMEM((kv, span + lanes, depth), bf16),
+            pltpu.VMEM((tokens, lanes), f32),
+        ],
+        cost_estimate=pl.CostEstimate(
+            flops=4 * tokens * heads * span * depth,
+            transcendentals=tokens * heads * span,
+            bytes_accessed=4 * span * kv * depth,
+        ),
+        name="attention",
+    )(
+        sc,
+        query_view,
+        cache_keys.reshape(span * kv, depth),
+        cached_value_rows.reshape(span * kv, depth),
+        incoming_keys.reshape(fresh * kv, depth),
+        incoming_values.reshape(fresh * kv, depth),
+    )
+    parts = local_call(
+        functools.partial(merge_rows_kernel, (heads, nc, fresh)),
+        [((fresh, wide), bf16)] * nc,
+        sc,
+        keep,
+        other_row(send),
+        name="merge_rows",
+    )
+    (attended,) = local_call(
+        functools.partial(merge_final_kernel, heads),
+        [((fresh, heads * lanes), bf16)],
+        sc,
+        *to_owners(parts),
+        name="merge_final",
+    )
+    (mixer_part,) = local_call(
+        functools.partial(mixer_project_kernel, (nc, nr, state_heads, channels)),
+        [((tokens, mixer_out.shape[1]), f32)],
+        sc,
+        gated_all,
+        gated_other,
+        mixer_out,
+        scratch=[pltpu.VMEM((state_heads * channels * nc * nr, tokens), bf16)],
+        name="mixer_project",
+    )
+    attended_all = jnp.concatenate(from_all(attended), axis=0)
+    columns = attention_out.shape[1]
+    keep, send = local_call(
+        functools.partial(branch_kernel, (nc, nr, fresh)),
+        [((half, columns), bf16)] * 2,
+        sc,
+        attended_all,
+        other_row(attended_all),
+        attention_out,
+        mixer_part,
+        name="branches",
+    )
+    parts = local_call(
+        functools.partial(side_by_side_kernel, (fresh, columns)),
+        [((fresh, nr * columns), bf16)] * nc,
+        sc,
+        keep,
+        other_row(send),
+        name="side_by_side",
+    )
+    model = residual.shape[1]
+    (branches,) = local_call(
+        functools.partial(columns_kernel, (nc, nr * columns)),
+        [((fresh, model), bf16)],
+        sc,
+        *to_owners(parts),
+        name="columns",
+    )
+    depth_in = hidden_gate.shape[0]
+    normed, trunk = local_call(
+        functools.partial(trunk_kernel, depth_in),
+        [((fresh, depth_in), bf16)] * 2,
+        sc,
+        residual,
+        branches,
+        other_head(branches),
+        norm_gain.reshape(1, model),
+        scratch=[pltpu.VMEM((fresh, model), bf16)] * 2,
+        name="trunk",
+    )
+    normed_all = jnp.concatenate(from_all(normed), axis=0)
+    normed_other = other_row(normed_all)
+
+    count = hidden_gate.shape[1]
+    unit = 3 * lanes
+    units = count // unit
+    sizes = [1] + [2] * ((units - 3) // 2) + [1] * (2 + (units - 3) % 2)
+    start = 0
+    mine, theirs = [], []
+    for size in sizes:
+        w = size * unit
+        kept, sent = gate_up(sc, normed_all, normed_other, hidden_gate, hidden_up, start, w, unit)
+        (hidden,) = local_call(
+            hidden_kernel, [((half, w), bf16)], sc, kept, other_head(sent), name="hidden"
+        )
+        mine.append(hidden)
+        theirs.append(other_head(hidden))
+        start += w
+    tail = sizes[-1] * unit
+    sums = down(sc, mine[:-1], theirs[:-1], hidden_down, 0, None, False)
+    keep, send = down(sc, mine[-1:], theirs[-1:], hidden_down, start - tail, sums, True)
+    own, *parts = local_call(
+        functools.partial(spread_kernel, fresh),
+        [((fresh, depth_in), f32)] + [((fresh, depth_in), bf16)] * (nc - 1),
+        sc,
+        keep,
+        other_row(send),
+        name="spread",
+    )
+    received = [shift(part, a + 1) for a, part in enumerate(parts)]
+    (out,) = local_call(
+        finish_kernel, [((fresh, depth_in), bf16)], sc, trunk, own, *received, name="finish"
+    )
+    return out
+
+
+def fits_small(mesh, args):
+    return mesh.shape["row"] == 2 and mesh.shape["head"] == 2 and mesh.shape["ctx"] <= 4
+
+
 def solution(mesh):
     in_specs = (
         P(("groups", "ctx", "row"), None),
@@ -217,6 +762,13 @@
         P(("ctx", "row"), "head"),
     )
     out_specs = P(("groups", "ctx", "row"), "head")
+    nc, nr, nh = mesh.shape["ctx"], mesh.shape["row"], mesh.shape["head"]
+
+    def on_device(*args):
+        if fits_small(mesh, args):
+            return small_form(nc, nr, nh, *args)
+        return general_form(*args)
+
     return jax.shard_map(
         on_device, mesh=mesh, in_specs=in_specs, out_specs=out_specs, check_vma=False
     )

time: 463 us -> 218 us (0.47)
  waiting for transfers between devices: 269 us -> 57.6 us
  Pallas kernels: 0 us -> 92.7 us
  matrix products: 77.1 us -> 4.65 us
  other arithmetic: 46.4 us -> 2.45 us
  starting transfers between devices: 4.85 us -> 43 us
  blocking collectives: 32.3 us -> 0 us
  between operations: 13.8 us -> 0.97 us
    all_gather x4 -> x0, waiting for transfers between devices: 114 us -> none  [the longest x1 67.8 us: combined_all(): gathered = jax.tree.map(lambda a: lax.all_gather(a, axis), part)]
    reduce_scatter x2 -> x0, waiting for transfers between devices: 106 us -> none  [the longest x1 68.2 us: on_device(): lax.psum_scatter(pair_partial, 'head', scatter_dimension=1, tiled=True)]
    pallas_call x0 -> x22, Pallas kernels: none -> 92.7 us  [the longest x14 32 us: local_call(): pl.pallas_call(kernel, out_shape=tuple((jax.ShapeDtypeStruct(s, d) for s,...]
    dot_general x15 -> x0, matrix products: 69.9 us -> none  [the longest x5 19.5 us: absorb(): jnp.einsum('kgts,skd->kgtd', weights.astype(jnp.bfloat16), block_values,...]
    ppermute x0 -> x35, waiting for transfers between devices: none -> 57.6 us  [the longest x18 42.9 us: shift(): return lax.ppermute(x, 'ctx', [(i, (i + by) % nc) for i in range(nc)])]
    ppermute x0 -> x35, starting transfers between devices: none -> 43 us  [the longest x18 30.2 us: shift(): return lax.ppermute(x, 'ctx', [(i, (i + by) % nc) for i in range(nc)])]
    all_gather x2 -> x0, blocking collectives: 32.3 us -> none  [combined_all(): gathered = jax.tree.map(lambda a: lax.all_gather(a, axis), part)]
    psum x1 -> x0, waiting for transfers between devices: 30 us -> none  [on_device(): summed = lax.psum(branches, 'head')]
  transfers between devices with their start and end apart: 8 -> 35, of which waited for: 7 -> 15; matrix products, arithmetic and copies ran while one was open for 15% -> 4% of each run, Pallas kernels for 0% -> 22%
where the time goes in v1:
time: 218 us; the launch traced here: 216 us
  Pallas kernels  92.7 us (43%)
  waiting for transfers between devices  57.6 us (26%)
  starting transfers between devices  43 us (20%)
  local copies, waits for them, and re-layouts  14.3 us (7%)
  matrix products  4.65 us (2%)
  other arithmetic  2.45 us (1%)
    ppermute x18, waiting for transfers between devices, shift(): return lax.ppermute(x, 'ctx', [(i, (i + by) % nc) for i in range(nc)])  42.9 us
    pallas_call x14, Pallas kernels, local_call(): pl.pallas_call(kernel, out_shape=tuple((jax.ShapeDtypeStruct(s, d) for s,...  32 us
    ppermute x18, starting transfers between devices, shift(): return lax.ppermute(x, 'ctx', [(i, (i + by) % nc) for i in range(nc)])  30.2 us
    pallas_call x5, Pallas kernels, gate_up(): pl.pallas_call(functools.partial(gate_up_kernel, unit), grid=(steps,), ou...  28 us
    pallas_call x1, Pallas kernels, small_form(): pl.pallas_call(functools.partial(attention_kernel, dims), grid=(heads,),...  17.5 us
    pallas_call x2, Pallas kernels, down(): pl.pallas_call(functools.partial(down_kernel, widths, first, last), grid=...  15.2 us
    unnamed x79, local copies, waits for them, and re-layouts  14.1 us
    ppermute x11, starting transfers between devices, other_head(): return lax.ppermute(x, 'head', [(i, (i + 1) % nh) for i in range(nh)])  11.6 us
  transfers between devices with their start and end apart: 35, of which 15 were waited for; matrix products, arithmetic and copies ran while one was open for 4% of the time, Pallas kernels for 22%

profile of v1, /device:TPU:0, one launch (start us, length us, event | category | flops | bytes accessed | tf_op | source)
XLA Modules:
  0.0 215.6 jit_solution(17099906176557434540)
XLA Ops:
  1.3 17.5 %attention.1 = (bf16[128,1408]{1,0:T(8,128)(2,1)}, bf16[128,1408]{1,0:T(8,128)(2,1)}) custom-call(s32[4]{0:T(128)} %pad_add_fusion.sc, bf16[10,8,32,128]{3,2,1,0:T(8,128)(2,1)} %bitcast.56, bf16[4096,128]{1,0:T(8,128)(2,1)} %bitcast.54, bf16[4096,128]{1,0:T(8,128)(2,1)} %bitcast.55, bf16[64,128]{1,0:T(8,128)(2,1)} %bitcast.57, bf16[64,128]{1,0:T(8,128)(2,1)} %bitcast.58), custom_call_target="tpu_custom_call" | custom-call | flops 2684354560 | bytes 2097152 | tf_op jit(solution)/shard_map/attention/pallas_call | solution.py:603
  20.6 4.1 %fusion.12 = f32[256,16,16]{0,2,1:T(8,128)S(1)} fusion(f32[256,256]{1,0:T(8,128)S(1)} %fusion.23, f32[16,256]{1,0:T(8,128)S(1)} %copy_bitcast_fusion, pred[256,256]{1,0:T(8,128)(4,1)S(1)} %iota_compare_fusion, bf16[256,16,16]{0,2,1:T(8,128)(2,1)S(1)} %copy-done.34, f32[256,16]{0,1:T(8,128)S(1)} %copy-done.33), kind=kOutput, calls=%fused_computation.13 | convolution fusion | flops 204603392 | bytes 753664 | tf_op jit(solution)/shard_map/hts,shp->thp/dot_general | solution.py:76
  25.4 3.0 %merge_rows.1 = (bf16[32,1408]{1,0:T(8,128)(2,1)}, bf16[32,1408]{1,0:T(8,128)(2,1)}, bf16[32,1408]{1,0:T(8,128)(2,1)}, bf16[32,1408]{1,0:T(8,128)(2,1)}) custom-call(s32[4]{0:T(128)} %pad_add_fusion.sc, bf16[128,1408]{1,0:T(8,128)(2,1)} %get-tuple-element.35.mine, bf16[128,1408]{1,0:T(8,128)(2,1)} %copy-done.10), custom_call_target="tpu_custom_call" | custom-call | tf_op jit(solution)/shard_map/merge_rows/pallas_call | solution.py:207
  28.4 2.6 %collective-permute-start.1 = (bf16[32,1408]{1,0:T(8,128)(2,1)}, bf16[32,1408]{1,0:T(8,128)(2,1)S(1)}, u32[]{:S(2)}, u32[]{:S(2)}) collective-permute-start(bf16[32,1408]{1,0:T(8,128)(2,1)} %get-tuple-element.38), channel_id=1, source_target_pairs={{0,4},{4,8},{8,12},{12,0},{1,5},{5,9},{9,13},{13,1},{2,6},{6,10},{... | collective-permute-start | bytes 270344 | tf_op jit(solution)/shard_map/ppermute | solution.py:577
  34.1 2.8 %collective-permute-start.8 = (bf16[256,256]{1,0:T(8,128)(2,1)S(1)}, bf16[256,256]{1,0:T(8,128)(2,1)S(1)}, u32[]{:S(2)}, u32[]{:S(2)}) collective-permute-start(bf16[256,256]{1,0:T(8,128)(2,1)S(1)} %bitcast.48), channel_id=1, source_target_pairs={{0,12},{4,0},{8,4},{12,8},{1,13},{5,1},{9,5},{13,9},{2,14},{6,2},{... | collective-permute-start | bytes 393224 | tf_op jit(solution)/shard_map/ppermute | solution.py:577
  38.8 13.0 %collective-permute-done.2.refs_2_ = bf16[32,1408]{1,0:T(8,128)(2,1)S(1)} collective-permute-done((bf16[32,1408]{1,0:T(8,128)(2,1)}, bf16[32,1408]{1,0:T(8,128)(2,1)S(1)}, u32[]{:S(2)}, u32[]{:S(2)}) %collective-permute-start.2) | collective-permute-done | bytes 90144 | tf_op jit(solution)/shard_map/ppermute | solution.py:577
  59.5 2.5 %collective-permute-done.6 = bf16[32,1280]{1,0:T(8,128)(2,1)S(1)} collective-permute-done((bf16[32,1280]{1,0:T(8,128)(2,1)}, bf16[32,1280]{1,0:T(8,128)(2,1)S(1)}, u32[]{:S(2)}, u32[]{:S(2)}) %collective-permute-start.6) | collective-permute-done | bytes 81952 | tf_op jit(solution)/shard_map/ppermute | solution.py:577
  62.0 2.6 %collective-permute-done.5 = bf16[32,1280]{1,0:T(8,128)(2,1)S(1)} collective-permute-done((bf16[32,1280]{1,0:T(8,128)(2,1)}, bf16[32,1280]{1,0:T(8,128)(2,1)S(1)}, u32[]{:S(2)}, u32[]{:S(2)}) %collective-permute-start.5) | collective-permute-done | bytes 81952 | tf_op jit(solution)/shard_map/ppermute | solution.py:577
  66.5 4.1 %mixer_project.1.mixer_part = f32[256,640]{1,0:T(8,128)} custom-call(s32[4]{0:T(128)} %pad_add_fusion.sc, bf16[4,256,256]{2,1,0:T(8,128)(2,1)} %copy-done.4, bf16[4,256,256]{2,1,0:T(8,128)(2,1)} %copy-done.7, bf16[2048,640]{1,0:T(8,128)(2,1)} %weight.2), custom_call_target="tpu_custom_call" | custom-call | tf_op jit(solution)/shard_map/mixer_project/pallas_call | solution.py:207
  71.4 3.1 %branches.1 = (bf16[128,640]{1,0:T(8,128)(2,1)}, bf16[128,640]{1,0:T(8,128)(2,1)}) custom-call(s32[4]{0:T(128)} %pad_add_fusion.sc, bf16[128,1280]{1,0:T(8,128)(2,1)} %copy-done.5, bf16[128,1280]{1,0:T(8,128)(2,1)} %copy-done.11, bf16[1280,640]{1,0:T(8,128)(2,1)} %weight.3, f32[256,640]{1,0:T(8,128)} %mixer_project.1.mixer_part), custom_call_target="tpu_custom_call" | custom-call | tf_op jit(solution)/shard_map/branches/pallas_call | solution.py:207
  83.1 2.9 %collective-permute-done.13.refs_1_ = bf16[32,1280]{1,0:T(8,128)(2,1)S(1)} collective-permute-done((bf16[32,1280]{1,0:T(8,128)(2,1)}, bf16[32,1280]{1,0:T(8,128)(2,1)S(1)}, u32[]{:S(2)}, u32[]{:S(2)}) %collective-permute-start.13) | collective-permute-done | bytes 81952 | tf_op jit(solution)/shard_map/ppermute | solution.py:577
  86.1 2.9 %collective-permute-done.14.refs_2_ = bf16[32,1280]{1,0:T(8,128)(2,1)S(1)} collective-permute-done((bf16[32,1280]{1,0:T(8,128)(2,1)}, bf16[32,1280]{1,0:T(8,128)(2,1)S(1)}, u32[]{:S(2)}, u32[]{:S(2)}) %collective-permute-start.14) | collective-permute-done | bytes 81952 | tf_op jit(solution)/shard_map/ppermute | solution.py:577
  92.9 8.3 %collective-permute-done.16.other = bf16[32,5120]{1,0:T(8,128)(2,1)S(1)} collective-permute-done((bf16[32,5120]{1,0:T(8,128)(2,1)}, bf16[32,5120]{1,0:T(8,128)(2,1)S(1)}, u32[]{:S(2)}, u32[]{:S(2)}) %collective-permute-start.16) | collective-permute-done | bytes 327712 | tf_op jit(solution)/shard_map/ppermute | solution.py:589
  109.8 6.9 %collective-permute-done.17 = bf16[32,2560]{1,0:T(8,128)(2,1)S(1)} collective-permute-done((bf16[32,2560]{1,0:T(8,128)(2,1)}, bf16[32,2560]{1,0:T(8,128)(2,1)S(1)}, u32[]{:S(2)}, u32[]{:S(2)}) %collective-permute-start.17) | collective-permute-done | bytes 163872 | tf_op jit(solution)/shard_map/ppermute | solution.py:577
  121.5 6.5 %gate_up.8 = (f32[2,128,768]{2,1,0:T(8,128)}, bf16[2,128,768]{2,1,0:T(8,128)(2,1)}) custom-call(s32[4]{0:T(128)} %pad_add_fusion.sc, bf16[128,2560]{1,0:T(8,128)(2,1)} %copy-done.2, bf16[128,2560]{1,0:T(8,128)(2,1)} %copy-done.3, bf16[2560,2688]{1,0:T(8,128)(2,1)} %gate.9, bf16[2560,2688]{1,0:T(8,128)(2,1)} %up.9), custom_call_target="tpu_custom_call" | custom-call | flops 2013265920 | bytes 7864320 | tf_op jit(solution)/shard_map/gate_up/pallas_call | solution.py:433
  129.6 6.6 %gate_up.7 = (f32[2,128,768]{2,1,0:T(8,128)}, bf16[2,128,768]{2,1,0:T(8,128)(2,1)}) custom-call(s32[4]{0:T(128)} %pad_add_fusion.sc, bf16[128,2560]{1,0:T(8,128)(2,1)} %copy-done.2, bf16[128,2560]{1,0:T(8,128)(2,1)} %copy-done.3, bf16[2560,2688]{1,0:T(8,128)(2,1)} %gate.9, bf16[2560,2688]{1,0:T(8,128)(2,1)} %up.9), custom_call_target="tpu_custom_call" | custom-call | flops 2013265920 | bytes 7864320 | tf_op jit(solution)/shard_map/gate_up/pallas_call | solution.py:433
  136.7 5.0 %gate_up.9 = (f32[2,128,384]{2,1,0:T(8,128)}, bf16[2,128,384]{2,1,0:T(8,128)(2,1)}) custom-call(s32[4]{0:T(128)} %pad_add_fusion.sc, bf16[128,2560]{1,0:T(8,128)(2,1)} %copy-done.2, bf16[128,2560]{1,0:T(8,128)(2,1)} %copy-done.3, bf16[2560,2688]{1,0:T(8,128)(2,1)} %gate.9, bf16[2560,2688]{1,0:T(8,128)(2,1)} %up.9), custom_call_target="tpu_custom_call" | custom-call | flops 1006632960 | bytes 3932160 | tf_op jit(solution)/shard_map/gate_up/pallas_call | solution.py:433
  143.1 5.0 %gate_up.6 = (f32[2,128,384]{2,1,0:T(8,128)}, bf16[2,128,384]{2,1,0:T(8,128)(2,1)}) custom-call(s32[4]{0:T(128)} %pad_add_fusion.sc, bf16[128,2560]{1,0:T(8,128)(2,1)} %copy-done.2, bf16[128,2560]{1,0:T(8,128)(2,1)} %copy-done.3, bf16[2560,2688]{1,0:T(8,128)(2,1)} %gate.9, bf16[2560,2688]{1,0:T(8,128)(2,1)} %up.9), custom_call_target="tpu_custom_call" | custom-call | flops 1006632960 | bytes 3932160 | tf_op jit(solution)/shard_map/gate_up/pallas_call | solution.py:433
  148.6 5.0 %gate_up.5 = (f32[2,128,384]{2,1,0:T(8,128)}, bf16[2,128,384]{2,1,0:T(8,128)(2,1)}) custom-call(s32[4]{0:T(128)} %pad_add_fusion.sc, bf16[128,2560]{1,0:T(8,128)(2,1)} %copy-done.2, bf16[128,2560]{1,0:T(8,128)(2,1)} %copy-done.3, bf16[2560,2688]{1,0:T(8,128)(2,1)} %gate.9, bf16[2560,2688]{1,0:T(8,128)(2,1)} %up.9), custom_call_target="tpu_custom_call" | custom-call | flops 1006632960 | bytes 3932160 | tf_op jit(solution)/shard_map/gate_up/pallas_call | solution.py:433
  175.0 9.3 %down.2.refs_3_ = f32[256,2560]{1,0:T(8,128)} custom-call(s32[4]{0:T(128)} %pad_add_fusion.sc, bf16[128,384]{1,0:T(8,128)(2,1)} %hidden.6.refs_0_, bf16[128,768]{1,0:T(8,128)(2,1)} %hidden.7.refs_1_, bf16[128,768]{1,0:T(8,128)(2,1)} %hidden.8.refs_2_, bf16[128,384]{1,0:T(8,128)(2,1)} %hidden.9.refs_3_, bf16[128,384]{1,0:T(8,128)(2,1)} %copy-done.25, ...), custom_call_target="tpu_custom_call" | custom-call | flops 3019898880 | bytes 11796480 | tf_op jit(solution)/shard_map/down/pallas_call | solution.py:507
  185.0 5.9 %down.3 = (f32[128,2560]{1,0:T(8,128)}, bf16[128,2560]{1,0:T(8,128)(2,1)}) custom-call(s32[4]{0:T(128)} %pad_add_fusion.sc, bf16[128,384]{1,0:T(8,128)(2,1)} %hidden.5.refs_0_, bf16[128,384]{1,0:T(8,128)(2,1)} %copy-done.26, bf16[2688,2560]{1,0:T(8,128)(2,1)} %refs_2_.1, f32[256,2560]{1,0:T(8,128)} %down.2.refs_3_), custom_call_target="tpu_custom_call" | custom-call | flops 503316480 | bytes 4587520 | tf_op jit(solution)/shard_map/down/pallas_call | solution.py:507
  196.5 4.0 %collective-permute-start.32 = (bf16[32,2560]{1,0:T(8,128)(2,1)}, bf16[32,2560]{1,0:T(8,128)(2,1)S(1)}, u32[]{:S(2)}, u32[]{:S(2)}) collective-permute-start(bf16[32,2560]{1,0:T(8,128)(2,1)} %get-tuple-element.62), channel_id=1, source_target_pairs={{0,4},{4,8},{8,12},{12,0},{1,5},{5,9},{9,13},{13,1},{2,6},{6,10},{... | collective-permute-start | bytes 491528 | tf_op jit(solution)/shard_map/ppermute | solution.py:577
  202.9 3.6 %collective-permute-done.32.refs_0_ = bf16[32,2560]{1,0:T(8,128)(2,1)S(1)} collective-permute-done((bf16[32,2560]{1,0:T(8,128)(2,1)}, bf16[32,2560]{1,0:T(8,128)(2,1)S(1)}, u32[]{:S(2)}, u32[]{:S(2)}) %collective-permute-start.32) | collective-permute-done | bytes 163872 | tf_op jit(solution)/shard_map/ppermute | solution.py:577
  206.4 6.5 %collective-permute-done.33.refs_1_ = bf16[32,2560]{1,0:T(8,128)(2,1)S(1)} collective-permute-done((bf16[32,2560]{1,0:T(8,128)(2,1)}, bf16[32,2560]{1,0:T(8,128)(2,1)S(1)}, u32[]{:S(2)}, u32[]{:S(2)}) %collective-permute-start.33) | collective-permute-done | bytes 163872 | tf_op jit(solution)/shard_map/ppermute | solution.py:577
  (163 shorter events, 80.9 us)
Async XLA Ops:
  28.4 8.9 %collective-permute-start.1 = (bf16[32,1408]{1,0:T(8,128)(2,1)}, bf16[32,1408]{1,0:T(8,128)(2,1)S(1)}, u32[]{:S(2)}, u32[]{:S(2)}) collective-permute-start(bf16[32,1408]{1,0:T(8,128)(2,1)} %get-tuple-element.38), channel_id=1, source_target_pairs={{0,4},{4,8},{8,12},{12,0},{1,5},{5,9},{9,13},{13,1},{2,6},{6,10},{... | collective-permute-start | bytes 270344 | tf_op jit(solution)/shard_map/ppermute | solution.py:577
  31.4 27.1 %collective-permute-start.10 = (bf16[256,256]{1,0:T(8,128)(2,1)S(1)}, bf16[256,256]{1,0:T(8,128)(2,1)S(1)}, u32[]{:S(2)}, u32[]{:S(2)}) collective-permute-start(bf16[256,256]{1,0:T(8,128)(2,1)S(1)} %bitcast.46), channel_id=1, source_target_pairs={{0,4},{4,8},{8,12},{12,0},{1,5},{5,9},{9,13},{13,1},{2,6},{6,10},{... | collective-permute-start | bytes 393224 | tf_op jit(solution)/shard_map/ppermute | solution.py:577
  33.1 26.3 %collective-permute-start.9 = (bf16[256,256]{1,0:T(8,128)(2,1)S(1)}, bf16[256,256]{1,0:T(8,128)(2,1)S(1)}, u32[]{:S(2)}, u32[]{:S(2)}) collective-permute-start(bf16[256,256]{1,0:T(8,128)(2,1)S(1)} %bitcast.47), channel_id=1, source_target_pairs={{0,8},{4,12},{8,0},{12,4},{1,9},{5,13},{9,1},{13,5},{2,10},{6,14},... | collective-permute-start | bytes 393224 | tf_op jit(solution)/shard_map/ppermute | solution.py:577
  34.1 25.2 %collective-permute-start.8 = (bf16[256,256]{1,0:T(8,128)(2,1)S(1)}, bf16[256,256]{1,0:T(8,128)(2,1)S(1)}, u32[]{:S(2)}, u32[]{:S(2)}) collective-permute-start(bf16[256,256]{1,0:T(8,128)(2,1)S(1)} %bitcast.48), channel_id=1, source_target_pairs={{0,12},{4,0},{8,4},{12,8},{1,13},{5,1},{9,5},{13,9},{2,14},{6,2},{... | collective-permute-start | bytes 393224 | tf_op jit(solution)/shard_map/ppermute | solution.py:577
  37.0 14.8 %collective-permute-start.2 = (bf16[32,1408]{1,0:T(8,128)(2,1)}, bf16[32,1408]{1,0:T(8,128)(2,1)S(1)}, u32[]{:S(2)}, u32[]{:S(2)}) collective-permute-start(bf16[32,1408]{1,0:T(8,128)(2,1)} %get-tuple-element.39), channel_id=1, source_target_pairs={{0,8},{4,12},{8,0},{12,4},{1,9},{5,13},{9,1},{13,5},{2,10},{6,14},... | collective-permute-start | bytes 270344 | tf_op jit(solution)/shard_map/ppermute | solution.py:577
  37.3 14.5 %collective-permute-start.3 = (bf16[32,1408]{1,0:T(8,128)(2,1)}, bf16[32,1408]{1,0:T(8,128)(2,1)S(1)}, u32[]{:S(2)}, u32[]{:S(2)}) collective-permute-start(bf16[32,1408]{1,0:T(8,128)(2,1)} %get-tuple-element.40), channel_id=1, source_target_pairs={{0,12},{4,0},{8,4},{12,8},{1,13},{5,1},{9,5},{13,9},{2,14},{6,2},{... | collective-permute-start | bytes 270344 | tf_op jit(solution)/shard_map/ppermute | solution.py:577
  56.9 7.6 %collective-permute-start.5 = (bf16[32,1280]{1,0:T(8,128)(2,1)}, bf16[32,1280]{1,0:T(8,128)(2,1)S(1)}, u32[]{:S(2)}, u32[]{:S(2)}) collective-permute-start(bf16[32,1280]{1,0:T(8,128)(2,1)} %merge_final.1), channel_id=1, source_target_pairs={{0,8},{4,12},{8,0},{12,4},{1,9},{5,13},{9,1},{13,5},{2,10},{6,14},... | collective-permute-start | bytes 245768 | tf_op jit(solution)/shard_map/ppermute | solution.py:577
  80.8 8.2 %collective-permute-start.14 = (bf16[32,1280]{1,0:T(8,128)(2,1)}, bf16[32,1280]{1,0:T(8,128)(2,1)S(1)}, u32[]{:S(2)}, u32[]{:S(2)}) collective-permute-start(bf16[32,1280]{1,0:T(8,128)(2,1)} %get-tuple-element.45), channel_id=1, source_target_pairs={{0,8},{4,12},{8,0},{12,4},{1,9},{5,13},{9,1},{13,5},{2,10},{6,14},... | collective-permute-start | bytes 245768 | tf_op jit(solution)/shard_map/ppermute | solution.py:577
  91.4 9.8 %collective-permute-start.16 = (bf16[32,5120]{1,0:T(8,128)(2,1)}, bf16[32,5120]{1,0:T(8,128)(2,1)S(1)}, u32[]{:S(2)}, u32[]{:S(2)}) collective-permute-start(bf16[32,5120]{1,0:T(8,128)(2,1)} %columns.1.mine), channel_id=1, source_target_pairs={{0,2},{2,0},{1,3},{3,1},{4,6},{6,4},{5,7},{7,5},{8,10},{10,8},{9,1... | collective-permute-start | bytes 983048 | tf_op jit(solution)/shard_map/ppermute | solution.py:589
  104.1 14.3 %collective-permute-start.19 = (bf16[32,2560]{1,0:T(8,128)(2,1)}, bf16[32,2560]{1,0:T(8,128)(2,1)S(1)}, u32[]{:S(2)}, u32[]{:S(2)}) collective-permute-start(bf16[32,2560]{1,0:T(8,128)(2,1)} %get-tuple-element.48), channel_id=1, source_target_pairs={{0,4},{4,8},{8,12},{12,0},{1,5},{5,9},{9,13},{13,1},{2,6},{6,10},{... | collective-permute-start | bytes 491528 | tf_op jit(solution)/shard_map/ppermute | solution.py:577
  106.4 12.0 %collective-permute-start.18 = (bf16[32,2560]{1,0:T(8,128)(2,1)}, bf16[32,2560]{1,0:T(8,128)(2,1)S(1)}, u32[]{:S(2)}, u32[]{:S(2)}) collective-permute-start(bf16[32,2560]{1,0:T(8,128)(2,1)} %get-tuple-element.48), channel_id=1, source_target_pairs={{0,8},{4,12},{8,0},{12,4},{1,9},{5,13},{9,1},{13,5},{2,10},{6,14},... | collective-permute-start | bytes 491528 | tf_op jit(solution)/shard_map/ppermute | solution.py:577
  106.4 10.2 %collective-permute-start.17 = (bf16[32,2560]{1,0:T(8,128)(2,1)}, bf16[32,2560]{1,0:T(8,128)(2,1)S(1)}, u32[]{:S(2)}, u32[]{:S(2)}) collective-permute-start(bf16[32,2560]{1,0:T(8,128)(2,1)} %get-tuple-element.48), channel_id=1, source_target_pairs={{0,12},{4,0},{8,4},{12,8},{1,13},{5,1},{9,5},{13,9},{2,14},{6,2},{... | collective-permute-start | bytes 491528 | tf_op jit(solution)/shard_map/ppermute | solution.py:577
  128.1 27.0 %collective-permute-start.25 = (bf16[2,128,768]{2,1,0:T(8,128)(2,1)}, bf16[2,128,768]{2,1,0:T(8,128)(2,1)S(1)}, u32[]{:S(2)}, u32[]{:S(2)}) collective-permute-start(bf16[2,128,768]{2,1,0:T(8,128)(2,1)} %get-tuple-element.56), channel_id=1, source_target_pairs={{0,2},{2,0},{1,3},{3,1},{4,6},{6,4},{5,7},{7,5},{8,10},{10,8},{9,1... | collective-permute-start | bytes 1179656 | tf_op jit(solution)/shard_map/ppermute | solution.py:589
  136.1 22.3 %collective-permute-start.24 = (bf16[2,128,768]{2,1,0:T(8,128)(2,1)}, bf16[2,128,768]{2,1,0:T(8,128)(2,1)S(1)}, u32[]{:S(2)}, u32[]{:S(2)}) collective-permute-start(bf16[2,128,768]{2,1,0:T(8,128)(2,1)} %get-tuple-element.54), channel_id=1, source_target_pairs={{0,2},{2,0},{1,3},{3,1},{4,6},{6,4},{5,7},{7,5},{8,10},{10,8},{9,1... | collective-permute-start | bytes 1179656 | tf_op jit(solution)/shard_map/ppermute | solution.py:589
  141.6 21.2 %collective-permute-start.26 = (bf16[2,128,384]{2,1,0:T(8,128)(2,1)}, bf16[2,128,384]{2,1,0:T(8,128)(2,1)S(1)}, u32[]{:S(2)}, u32[]{:S(2)}) collective-permute-start(bf16[2,128,384]{2,1,0:T(8,128)(2,1)} %get-tuple-element.58), channel_id=1, source_target_pairs={{0,2},{2,0},{1,3},{3,1},{4,6},{6,4},{5,7},{7,5},{8,10},{10,8},{9,1... | collective-permute-start | bytes 589832 | tf_op jit(solution)/shard_map/ppermute | solution.py:589
  148.1 17.8 %collective-permute-start.23 = (bf16[2,128,384]{2,1,0:T(8,128)(2,1)}, bf16[2,128,384]{2,1,0:T(8,128)(2,1)S(1)}, u32[]{:S(2)}, u32[]{:S(2)}) collective-permute-start(bf16[2,128,384]{2,1,0:T(8,128)(2,1)} %get-tuple-element.52), channel_id=1, source_target_pairs={{0,2},{2,0},{1,3},{3,1},{4,6},{6,4},{5,7},{7,5},{8,10},{10,8},{9,1... | collective-permute-start | bytes 589832 | tf_op jit(solution)/shard_map/ppermute | solution.py:589
  153.6 16.2 %collective-permute-start.21 = (bf16[2,128,384]{2,1,0:T(8,128)(2,1)}, bf16[2,128,384]{2,1,0:T(8,128)(2,1)S(1)}, u32[]{:S(2)}, u32[]{:S(2)}) collective-permute-start(bf16[2,128,384]{2,1,0:T(8,128)(2,1)} %get-tuple-element.50), channel_id=1, source_target_pairs={{0,2},{2,0},{1,3},{3,1},{4,6},{6,4},{5,7},{7,5},{8,10},{10,8},{9,1... | collective-permute-start | bytes 589832 | tf_op jit(solution)/shard_map/ppermute | solution.py:589
  157.9 15.7 %collective-permute-start.29 = (bf16[128,768]{1,0:T(8,128)(2,1)}, bf16[128,768]{1,0:T(8,128)(2,1)S(1)}, u32[]{:S(2)}, u32[]{:S(2)}) collective-permute-start(bf16[128,768]{1,0:T(8,128)(2,1)} %hidden.8.refs_2_), channel_id=1, source_target_pairs={{0,2},{2,0},{1,3},{3,1},{4,6},{6,4},{5,7},{7,5},{8,10},{10,8},{9,1... | collective-permute-start | bytes 589832 | tf_op jit(solution)/shard_map/ppermute | solution.py:589
  161.3 12.3 %collective-permute-start.28 = (bf16[128,768]{1,0:T(8,128)(2,1)}, bf16[128,768]{1,0:T(8,128)(2,1)S(1)}, u32[]{:S(2)}, u32[]{:S(2)}) collective-permute-start(bf16[128,768]{1,0:T(8,128)(2,1)} %hidden.7.refs_1_), channel_id=1, source_target_pairs={{0,2},{2,0},{1,3},{3,1},{4,6},{6,4},{5,7},{7,5},{8,10},{10,8},{9,1... | collective-permute-start | bytes 589832 | tf_op jit(solution)/shard_map/ppermute | solution.py:589
  165.3 7.5 %collective-permute-start.30 = (bf16[128,384]{1,0:T(8,128)(2,1)}, bf16[128,384]{1,0:T(8,128)(2,1)S(1)}, u32[]{:S(2)}, u32[]{:S(2)}) collective-permute-start(bf16[128,384]{1,0:T(8,128)(2,1)} %hidden.9.refs_3_), channel_id=1, source_target_pairs={{0,2},{2,0},{1,3},{3,1},{4,6},{6,4},{5,7},{7,5},{8,10},{10,8},{9,1... | collective-permute-start | bytes 294920 | tf_op jit(solution)/shard_map/ppermute | solution.py:589
  172.3 12.1 %collective-permute-start.22 = (bf16[128,384]{1,0:T(8,128)(2,1)}, bf16[128,384]{1,0:T(8,128)(2,1)S(1)}, u32[]{:S(2)}, u32[]{:S(2)}) collective-permute-start(bf16[128,384]{1,0:T(8,128)(2,1)} %hidden.5.refs_0_), channel_id=1, source_target_pairs={{0,2},{2,0},{1,3},{3,1},{4,6},{6,4},{5,7},{7,5},{8,10},{10,8},{9,1... | collective-permute-start | bytes 294920 | tf_op jit(solution)/shard_map/ppermute | solution.py:589
  196.5 10.0 %collective-permute-start.32 = (bf16[32,2560]{1,0:T(8,128)(2,1)}, bf16[32,2560]{1,0:T(8,128)(2,1)S(1)}, u32[]{:S(2)}, u32[]{:S(2)}) collective-permute-start(bf16[32,2560]{1,0:T(8,128)(2,1)} %get-tuple-element.62), channel_id=1, source_target_pairs={{0,4},{4,8},{8,12},{12,0},{1,5},{5,9},{9,13},{13,1},{2,6},{6,10},{... | collective-permute-start | bytes 491528 | tf_op jit(solution)/shard_map/ppermute | solution.py:577
  200.5 12.4 %collective-permute-start.33 = (bf16[32,2560]{1,0:T(8,128)(2,1)}, bf16[32,2560]{1,0:T(8,128)(2,1)S(1)}, u32[]{:S(2)}, u32[]{:S(2)}) collective-permute-start(bf16[32,2560]{1,0:T(8,128)(2,1)} %get-tuple-element.63), channel_id=1, source_target_pairs={{0,8},{4,12},{8,0},{12,4},{1,9},{5,13},{9,1},{13,5},{2,10},{6,14},... | collective-permute-start | bytes 491528 | tf_op jit(solution)/shard_map/ppermute | solution.py:577
  201.7 11.3 %collective-permute-start.34 = (bf16[32,2560]{1,0:T(8,128)(2,1)}, bf16[32,2560]{1,0:T(8,128)(2,1)S(1)}, u32[]{:S(2)}, u32[]{:S(2)}) collective-permute-start(bf16[32,2560]{1,0:T(8,128)(2,1)} %get-tuple-element.64), channel_id=1, source_target_pairs={{0,12},{4,0},{8,4},{12,8},{1,13},{5,1},{9,5},{13,9},{2,14},{6,2},{... | collective-permute-start | bytes 491528 | tf_op jit(solution)/shard_map/ppermute | solution.py:577
  (49 other events, 290.1 us)
